TPU v7x, 128 devices: a whole 4x4x4 slice. The times are simulated.
128 devices in a mesh: rep: 16 (over x, y_lo, core), shard: 8 (over y_hi, z).
Axes of the slice: x: 4, y: 4 (y_hi: 2, y_lo: 2; y = y_hi * 2 + y_lo), z: 4, core: 2. Of those that a mesh axis runs over, the one named last changes fastest.
Arguments:
- x_in: bfloat16 [40960, 1024], P(('rep', 'shard')), may hold values from -6 to 6
- cotangent: float32 [40960, 1024], P(('rep', 'shard')), may hold values from -24 to 24
- ln1_gain: bfloat16 [1024], P('shard'), may hold values from 0.5 to 1.5
- ln1_bias: bfloat16 [1024], P('shard'), may hold values from -3 to 3
- w_qkv: bfloat16 [1024, 3072], P('shard'), may hold values from -8 to 8
- q_bias: bfloat16 [1024], P('shard'), may hold values from -3 to 3
- v_bias: bfloat16 [1024], P('shard'), may hold values from -3 to 3
- w_attn_out: bfloat16 [1024, 1024], P('shard'), may hold values from -0.75 to 0.75
- out_bias: bfloat16 [1024], P('shard'), may hold values from -3 to 3
- ln2_gain: bfloat16 [1024], P('shard'), may hold values from 0.5 to 1.5
- ln2_bias: bfloat16 [1024], P('shard'), may hold values from -3 to 3
- w_up: bfloat16 [1024, 4096], P('shard'), may hold values from -0.1875 to 0.1875
- up_bias: bfloat16 [4096], P('shard'), may hold values from -3 to 3
- w_down: bfloat16 [4096, 1024], P('shard'), may hold values from -0.09375 to 0.09375
- down_bias: bfloat16 [1024], P('shard'), may hold values from -3 to 3
Outputs:
- block_out: bfloat16 [40960, 1024], P(('rep', 'shard'))
- input_grad: float32 [40960, 1024], P(('rep', 'shard'))
- grad_ln1_gain: float32 [1024], P('shard')
- grad_ln1_bias: float32 [1024], P('shard')
- grad_w_qkv: float32 [1024, 3072], P('shard')
- grad_q_bias: float32 [1024], P('shard')
- grad_v_bias: float32 [1024], P('shard')
- grad_w_attn_out: float32 [1024, 1024], P('shard')
- grad_out_bias: float32 [1024], P('shard')
- grad_ln2_gain: float32 [1024], P('shard')
- grad_ln2_bias: float32 [1024], P('shard')
- grad_w_up: float32 [1024, 4096], P('shard')
- grad_up_bias: float32 [4096], P('shard')
- grad_w_down: float32 [4096, 1024], P('shard')
- grad_down_bias: float32 [1024], P('shard')
All inputs are finite; a program needn't handle non-finite values.
Results may differ from a plain program's by a relative error of at most 0.023.
Values may be sent and summed in bfloat16 or wider, within the bound.
A program may use at most 192 MiB of HBM per device.

v0:
```python
import math

import jax
import jax.numpy as jnp
from jax import lax
from jax.experimental import pallas as pl
from jax.experimental.pallas import tpu as pltpu
from jax.sharding import PartitionSpec as P

HEADS = 16
HEAD_DIM = 64
SEQ = 320
D = 1024
NCH = 12
MESH = pl.DeviceIdType.MESH
BF16 = jnp.bfloat16
F32 = jnp.float32
MIB = 1024 * 1024

eps_norm = 1e-05
sqrt_two_pi = math.sqrt(2.0 / math.pi)
cubic_coef = 0.044715

LN1G, LN1B, QB, VB, OB, LN2G, LN2B, DB, UB = 0, 1, 2, 3, 4, 5, 6, 7, 8
WQ, WK, WV, WO, WUP, WDN = 0, 1, 2, 3, 4, 8


def place():
    rep = lax.axis_index("rep")
    shard = lax.axis_index("shard")
    x, lo, core = rep // 4, (rep // 2) % 2, rep % 2
    hi, z = shard // 4, shard % 4

    def dev(x_, lo_, core_, hi_, z_):
        return ((x_ * 2 + lo_) * 2 + core_, hi_ * 4 + z_)

    peers = dict(
        xr=dev((x + 1) % 4, lo, core, hi, z),
        xl=dev((x + 3) % 4, lo, core, hi, z),
        xo=dev((x + 2) % 4, lo, core, hi, z),
        zr=dev(x, lo, core, hi, (z + 1) % 4),
        zl=dev(x, lo, core, hi, (z + 3) % 4),
        zo=dev(x, lo, core, hi, (z + 2) % 4),
        cross=dev(x, 1 - lo, core, 1 - hi, z),
        ylo=dev(x, 1 - lo, core, hi, z),
        yo=dev(x, lo, core, 1 - hi, z),
        core=dev(x, lo, 1 - core, hi, z),
    )
    return x, core, hi, z, peers


def greet(peers, names):
    barrier = pltpu.get_barrier_semaphore()
    for name in names:
        pl.semaphore_signal(barrier, inc=1, device_id=peers[name], device_id_type=MESH)
    pl.semaphore_wait(barrier, len(names))


def loop(n, body):
    def step(i, carry):
        body(i)
        return carry

    lax.fori_loop(0, n, step, 0)


def rows_of(i, n):
    return pl.ds(pl.multiple_of(i * n, n), n)


def nn(a, b):
    return jnp.dot(a, b, preferred_element_type=F32)


def nt(a, b):
    return lax.dot_general(a, b, (((1,), (1,)), ((), ())), preferred_element_type=F32)


def tn(a, b):
    return lax.dot_general(a, b, (((0,), (0,)), ((), ())), preferred_element_type=F32)


def slope_of(h):
    return 2.0 ** (-8.0 * (h + 1) / HEADS)


def gelu_both(u):
    tanh_val = jnp.tanh(sqrt_two_pi * (u + cubic_coef * u * u * u))
    value = 0.5 * u * (1.0 + tanh_val)
    slope = 0.5 * (1.0 + tanh_val) + 0.5 * u * (1.0 - tanh_val * tanh_val) * sqrt_two_pi * (
        1.0 + 3.0 * cubic_coef * u * u
    )
    return value, slope


def center_scale(rows):
    c = rows - jnp.mean(rows, axis=-1, keepdims=True)
    s = lax.rsqrt(jnp.mean(c * c, axis=-1, keepdims=True) + eps_norm)
    return c * s, s


HALF = 512
NH = 24
GCOPIES = 20
GAP = 3


def forward_kernel(*refs):
    w_qkv, w_o, w_up, w_down, small, x_in = refs[:6]
    full_out, sm_all, block_out, act1_o, qkv_o, lse, ctx_o, act2_o, n2_o, hid_o, slope_o = refs[6:17]
    full, act1, qkv, ctx, act2, n2, hid, slope, mid, dist, vecs, qkv_bias = refs[17:29]
    send_sem, recv_sem, own_sem, out_sem, sm_send, sm_recv, save_sem = refs[29:]
    x, core, hi, z, peers = place()
    other = 1 - hi
    me = hi * 4 + z
    left, right, far = hi * 4 + (z + 3) % 4, hi * 4 + (z + 1) % 4, hi * 4 + (z + 2) % 4

    def own(src, m, cols):
        pltpu.make_async_copy(src, full.at[m, me, :, cols], own_sem.at[m]).start()

    wide = pl.ds(0, D)
    for c in range(3):
        own(w_qkv.at[:, pl.ds(c * D, D)], WQ + c, wide)
    own(w_o, WO, wide)
    for j in range(4):
        for s in range(8):
            own(w_up.at[:, pl.ds(s * 512 + j * 128, 128)], WUP + j, pl.ds(s * 128, 128))
    for j in range(4):
        own(w_down.at[pl.ds(j * 128, 128)], WDN + j, wide)
    sm_all[me] = small[...]
    greet(peers, ("xr", "xl", "zr", "zl", "cross", "core"))

    def remote(src, dst, ss, rs, to):
        return pltpu.make_async_remote_copy(
            src_ref=src,
            dst_ref=dst,
            send_sem=ss,
            recv_sem=rs,
            device_id=peers[to],
            device_id_type=MESH,
        )

    base, quarter = core * 64, core * 64 + x * 16
    others = pl.ds(other * 4, 4)
    sx = lambda i: base + ((x + i) % 4) * 16

    def copies(k):
        cols = pl.ds(pl.multiple_of((k % 2) * HALF, HALF), HALF)

        def view(which, first, count):
            return full.at[k // 2, which, pl.ds(pl.multiple_of(first, 16), count), cols]

        table = (
            ("z1r", view(me, base, 64), "zr"),
            ("z1l", view(me, base, 64), "zl"),
            ("y0", view(me, quarter, 16), "cross"),
            ("z2r", view(left, base, 32), "zr"),
            ("y1", view(left, quarter, 16), "cross"),
            ("c1", view(left, base, 64), "core"),
            ("z2l", view(right, base + 32, 32), "zl"),
            ("y2", view(right, quarter, 16), "cross"),
            ("c2", view(right, base, 64), "core"),
            ("y3", view(far, quarter, 16), "cross"),
            ("c3", view(far, base, 64), "core"),
            ("x1r", view(others, quarter, 16), "xr"),
            ("x1l", view(others, quarter, 16), "xl"),
            ("c4", view(others, quarter, 16), "core"),
            ("x2r", view(pl.ds(other * 4, 2), sx(3), 16), "xr"),
            ("c5", view(others, sx(3), 16), "core"),
            ("x2l", view(pl.ds(other * 4 + 2, 2), sx(1), 16), "xl"),
            ("c6", view(others, sx(1), 16), "core"),
            ("c7", view(others, sx(2), 16), "core"),
        )
        return {
            name: remote(v, v, send_sem.at[k, i], recv_sem.at[k, i], to)
            for i, (name, v, to) in enumerate(table)
        }

    def stage(waits, sends):
        def run(k):
            c = copies(k)
            for name in waits:
                c[name].wait_recv()
            for name in sends:
                c[name].start()

        return run

    def stage0(k):
        @pl.when(k % 2 == 0)
        def _():
            mine = full.at[k // 2, me]
            pltpu.make_async_copy(mine, mine, own_sem.at[k // 2]).wait()

        stage((), ("z1r", "z1l", "y0"))(k)

    def stage1(k):
        stage(("z1r",), ("z2r", "y1", "c1"))(k)
        stage(("z1l",), ("z2l", "y2", "c2"))(k)

    def stage4(k):
        stage(("x1r",), ("x2r", "c5"))(k)
        stage(("x1l",), ("x2l", "c6"))(k)

    def keep(m):
        return pltpu.make_async_copy(full.at[m], full_out.at[m], out_sem.at[m])

    def stage6(k):
        stage(("c1", "c2", "c3", "c4", "c5", "c6", "c7"), ())(k)

        @pl.when(k % 2 == 1)
        def _():
            keep(k // 2).start()

    stages = (
        stage0,
        stage1,
        stage(("z2r", "z2l"), ("y3", "c3")),
        stage(("y0", "y1", "y2", "y3"), ("x1r", "x1l", "c4")),
        stage4,
        stage(("x2r", "x2l"), ("c7",)),
        stage6,
    )

    def comm(t):
        for s in range(6, -1, -1):
            k = t - GAP * s

            @pl.when((k >= 0) & (k < NH))
            def _():
                stages[s](k)

    sm_copy = [
        remote(sm_all.at[me], sm_all.at[me], sm_send.at[0], sm_recv.at[0], "zr"),
        remote(sm_all.at[me], sm_all.at[me], sm_send.at[1], sm_recv.at[1], "zl"),
        remote(sm_all.at[left], sm_all.at[left], sm_send.at[2], sm_recv.at[2], "zr"),
        remote(sm_all.at[pl.ds(hi * 4, 4)], sm_all.at[pl.ds(hi * 4, 4)], sm_send.at[3], sm_recv.at[3], "cross"),
    ]

    def vec(i):
        return vecs[i : i + 1, :]

    def save(i, src, dst):
        return pltpu.make_async_copy(src, dst, save_sem.at[i])

    saves = [
        save(0, act1, act1_o),
        save(1, qkv, qkv_o),
        save(2, ctx, ctx_o),
        save(3, act2, act2_o),
        save(4, n2, n2_o),
    ]

    def norm_one():
        for s in range(8):
            vecs[:, pl.ds(s * 128, 128)] = sm_all[s].astype(F32)
        qkv_bias[0:1, :] = vec(QB)
        qkv_bias[1:2, :] = jnp.zeros((1, D), F32)
        qkv_bias[2:3, :] = vec(VB)

        def body(i):
            r = rows_of(i, 32)
            n, s = center_scale(x_in[r, :].astype(F32))
            act1[r, :] = (n * vec(LN1G) + vec(LN1B)).astype(BF16)

        loop(10, body)
        row = lax.broadcasted_iota(jnp.int32, (SEQ, SEQ), 0)
        col = lax.broadcasted_iota(jnp.int32, (SEQ, SEQ), 1)
        dist[...] = (row - col).astype(F32)
        saves[0].start()

    def matmul(a_ref, k, write):
        def body(i):
            cols = pl.ds(pl.multiple_of((k % 2) * HALF + i * 256, 256), 256)
            write(cols, nn(a_ref[...], full[k // 2, :, :, cols].reshape(D, 256)))

        loop(2, body)

    def project(k):
        def write(cols, res):
            qkv[k // 2, :, cols] = (res + qkv_bias[pl.ds(k // 2, 1), cols]).astype(BF16)

        matmul(act1, k, write)

    def attend(p, factor):
        cols = pl.ds(pl.multiple_of(p * 128, 128), 128)
        lane = lax.broadcasted_iota(jnp.int32, (SEQ, 128), 1)
        q_pair, k_pair, v_pair = qkv[0, :, cols], qkv[1, :, cols], qkv[2, :, cols]
        out = []
        lse_all = lse[...]
        for e in range(2):
            mine = (lane < 64) if e == 0 else (lane >= 64)
            s = nt(jnp.where(mine, q_pair, jnp.zeros_like(q_pair)), k_pair)
            d = dist[...]
            s = jnp.where(d >= 0.0, s * HEAD_DIM**-0.5 - (factor * slope_of(e)) * d, -jnp.inf)
            top = jnp.max(s, axis=-1, keepdims=True)
            s = jnp.exp(s - top)
            total = jnp.sum(s, axis=-1, keepdims=True)
            lse_all = jnp.where(lane == 2 * p + e, top + jnp.log(total), lse_all)
            out.append(nn((s / total).astype(BF16), v_pair))
        lse[...] = lse_all
        ctx[:, cols] = jnp.where(lane < 64, out[0], out[1]).astype(BF16)
        return factor * 0.5

    def attend_half(i):
        @pl.when(i == 0)
        def _():
            lse[...] = jnp.zeros_like(lse)
            saves[1].start()

        first = jnp.where(i == 0, 1.0, 0.0625).astype(F32)
        lax.fori_loop(0, 4, lambda p, f: attend(i * 4 + p, f), first)

    def out_proj():
        saves[2].start()

        def body(k):
            def write(cols, res):
                mid[:, cols] = res + vecs[OB : OB + 1, cols] + x_in[:, cols].astype(F32)

            matmul(ctx, 2 * WO + k, write)

        loop(2, body)

        def norm(i):
            r = rows_of(i, 32)
            n, s = center_scale(mid[r, :])
            n2[r, pl.ds(0, D)] = n
            n2[r, pl.ds(D, 128)] = jnp.broadcast_to(s, (32, 128))
            act2[r, :] = (n * vec(LN2G) + vec(LN2B)).astype(BF16)

        loop(10, norm)
        saves[3].start()
        saves[4].start()

    def save_up(j):
        return (
            pltpu.make_async_copy(hid.at[j], hid_o.at[j], save_sem.at[5 + j]),
            pltpu.make_async_copy(slope.at[j], slope_o.at[j], save_sem.at[9 + j]),
        )

    def up(k):
        j = k // 2 - WUP

        def write(cols, res):
            value, grad = gelu_both(res + vecs[pl.ds(UB + j, 1), cols])
            hid[j, :, cols] = value.astype(BF16)
            slope[j, :, cols] = grad

        matmul(act2, k, write)

        @pl.when(k % 2 == 1)
        def _():
            for cp in save_up(j):
                cp.start()

    def down(k):
        j = k // 2 - WDN

        def write(cols, res):
            res = res + mid[:, cols]

            @pl.when(j < 3)
            def _():
                mid[:, cols] = res

            @pl.when(j == 3)
            def _():
                block_out[:, cols] = (res + vecs[DB : DB + 1, cols]).astype(BF16)

        matmul(hid.at[j], k, write)

    sm_copy[0].start()
    sm_copy[1].start()

    def slot(t):
        comm(t)

        @pl.when(t == 2)
        def _():
            sm_copy[0].wait_recv()
            sm_copy[1].wait_recv()
            sm_copy[2].start()

        @pl.when(t == 4)
        def _():
            sm_copy[2].wait_recv()
            sm_copy[3].start()

        @pl.when(t == 6)
        def _():
            sm_copy[3].wait_recv()
            norm_one()

        k = t - 6 * GAP

        @pl.when((k >= 0) & (k < 6))
        def _():
            project(k)

        @pl.when((k >= 6) & (k < 8))
        def _():
            attend_half(k - 6)

        @pl.when(k == 7)
        def _():
            out_proj()

        @pl.when((k >= 8) & (k < 16))
        def _():
            up(k)

        @pl.when(k >= 16)
        def _():
            down(k)

    loop(NH + 6 * GAP, slot)

    def sent(k):
        for cp in copies(k).values():
            cp.wait_send()

    loop(NH, sent)
    for cp in sm_copy:
        cp.wait_send()
    for m in range(NCH):
        keep(m).wait()
    for cp in saves:
        cp.wait()
    for j in range(4):
        for cp in save_up(j):
            cp.wait()


def gather_forward(w_qkv, w_attn_out, w_up, w_down, small, x_in):
    vm = pl.BlockSpec(memory_space=pltpu.VMEM)
    hbm = pl.BlockSpec(memory_space=pl.ANY)
    S = jax.ShapeDtypeStruct
    V = pltpu.VMEM
    dma = pltpu.SemaphoreType.DMA
    act = S((SEQ, D), BF16)
    return pl.pallas_call(
        forward_kernel,
        out_shape=[
            S((NCH, 8, 128, D), BF16),
            S((8, 16, 128), BF16),
            act,
            act,
            S((3, SEQ, D), BF16),
            S((SEQ, 128), F32),
            act,
            act,
            S((SEQ, D + 128), F32),
            S((4, SEQ, D), BF16),
            S((4, SEQ, D), F32),
        ],
        in_specs=[hbm] * 4 + [vm] * 2,
        out_specs=[hbm, vm, vm, hbm, hbm, vm, hbm, hbm, hbm, hbm, hbm],
        scratch_shapes=[
            V((NCH, 8, 128, D), BF16),
            V((SEQ, D), BF16),
            V((3, SEQ, D), BF16),
            V((SEQ, D), BF16),
            V((SEQ, D), BF16),
            V((SEQ, D + 128), F32),
            V((4, SEQ, D), BF16),
            V((4, SEQ, D), F32),
            V((SEQ, D), F32),
            V((SEQ, SEQ), F32),
            V((16, D), F32),
            V((8, D), F32),
            dma((NH, GCOPIES)),
            dma((NH, GCOPIES)),
            dma((NCH,)),
            dma((NCH,)),
            dma((4,)),
            dma((4,)),
            dma((13,)),
        ],
        compiler_params=pltpu.CompilerParams(
            collective_id=0, has_side_effects=True, vmem_limit_bytes=60 * MIB
        ),
        name="gather_forward",
    )(w_qkv, w_attn_out, w_up, w_down, small, x_in)


RCOPIES = 20
STAGED = 4
WSLOTS = 3
RGAP = 2
MADE = (
    [(m + j, h) for j in range(4) for m in (WDN, WUP) for h in range(2)]
    + [(WO, 0), (WO, 1)]
    + [(m, h) for h in range(2) for m in (WV, WK, WQ)]
)


def backward_kernel(*refs):
    full, hid_hbm, slope_hbm, sm_all, x_in, cot, act1, qkv, lse, ctx, act2, n2 = refs[:12]
    input_grad, out_qkv, out_o, out_up, out_down, fin_small = refs[12:18]
    acc, staged, rx1, rx2, ry, rz1, rz2, rp1, rp2, fin = refs[18:28]
    wbuf, hid_buf, slope_buf, cot_b, dub, dact, dmid, dmid_b, dctx, dqkv, dist, vecs = refs[28:40]
    sums, small_in = refs[40:42]
    send_sem, recv_sem, load_sem, hid_sem, sm_send, sm_recv = refs[42:]
    x, core, hi, z, peers = place()
    lo = (lax.axis_index("rep") // 2) % 2
    other = 1 - hi
    me = hi * 4 + z
    xp, xm, xo = (x + 1) % 4, (x + 3) % 4, (x + 2) % 4
    zp, zm, zo = (z + 1) % 4, (z + 3) % 4, (z + 2) % 4
    others = pl.ds(other * 4, 4)

    def remote(src, dst, ss, rs, to):
        return pltpu.make_async_remote_copy(
            src_ref=src,
            dst_ref=dst,
            send_sem=ss,
            recv_sem=rs,
            device_id=peers[to],
            device_id_type=MESH,
        )

    def sub(i):
        return pl.ds(pl.multiple_of(i * 16, 16), 16)

    def block(i):
        return pl.ds(pl.multiple_of(i * 128, 128), 128)

    def fin_rows(lo_):
        return pl.ds(pl.multiple_of(core * 64 + lo_ * 32, 32), 32)

    mine32 = pl.ds(pl.multiple_of(lo * 32, 32), 32)
    theirs32 = pl.ds(pl.multiple_of((1 - lo) * 32, 32), 32)

    def copies(k):
        piece = fin.at[k, fin_rows(lo), block(x)]
        whole = fin.at[k, fin_rows(lo)]
        theirs = fin.at[k, fin_rows(1 - lo)]
        table = (
            ("c", staged.at[k % STAGED, 1 - core], acc.at[k], "core"),
            ("x1r", acc.at[k, pl.ds(other * 4, 2), sub(xo)], rx1.at[k, 0], "xr"),
            ("x1l", acc.at[k, pl.ds(other * 4 + 2, 2), sub(xo)], rx1.at[k, 1], "xl"),
            ("x2r", acc.at[k, others, sub(xp)], rx2.at[k, 0], "xr"),
            ("x2l", acc.at[k, others, sub(xm)], rx2.at[k, 1], "xl"),
            ("y", acc.at[k, others, sub(x)], ry.at[k], "cross"),
            ("z1r", acc.at[k, hi * 4 + zo, pl.ds(0, 32)], rz1.at[k, 0], "zr"),
            ("z1l", acc.at[k, hi * 4 + zo, pl.ds(32, 32)], rz1.at[k, 1], "zl"),
            ("z2r", acc.at[k, hi * 4 + zp], rz2.at[k, 0], "zr"),
            ("z2l", acc.at[k, hi * 4 + zm], rz2.at[k, 1], "zl"),
            ("p1", acc.at[k, me, theirs32], rp1.at[k], "ylo"),
            ("p2r", acc.at[k, me, mine32, block(xp)], rp2.at[k, 0], "xr"),
            ("p2l", acc.at[k, me, mine32, block(xm)], rp2.at[k, 1], "xl"),
            ("p2o", acc.at[k, me, mine32, block(xo)], rp2.at[k, 2], "xo"),
            ("p3r", piece, piece, "xr"),
            ("p3l", piece, piece, "xl"),
            ("p3o", piece, piece, "xo"),
            ("p4y", whole, whole, "ylo"),
            ("p4c", whole, whole, "core"),
            ("p5", theirs, theirs, "core"),
        )
        return {
            name: remote(src, dst, send_sem.at[k, i], recv_sem.at[k, i], to)
            for i, (name, src, dst, to) in enumerate(table)
        }

    def got(c, *names):
        for name in names:
            c[name].wait_recv()

    def go(c, *names):
        for name in names:
            c[name].start()

    def add(idx, *terms):
        total = acc[idx].astype(F32)
        for ref, i in terms:
            total = total + ref[i].astype(F32)
        acc[idx] = total.astype(BF16)

    def s0(k):
        c = copies(k)
        got(c, "c")

        def body(i):
            add((k, i), (staged, (k % STAGED, core, i)))

        loop(8, body)
        go(c, "x1r", "x1l")

    def s1(k):
        c = copies(k)
        got(c, "x1r", "x1l")
        add((k, pl.ds(other * 4, 2), sub(xp)), (rx1, (k, 0)))
        go(c, "x2r")
        add((k, pl.ds(other * 4 + 2, 2), sub(xm)), (rx1, (k, 1)))
        go(c, "x2l")

    def s2(k):
        c = copies(k)
        got(c, "x2r", "x2l")
        add((k, others, sub(x)), (rx2, (k, 0)), (rx2, (k, 1)))
        go(c, "y")

    def s3(k):
        c = copies(k)
        got(c, "y")
        add((k, pl.ds(hi * 4, 4), sub(x)), (ry, (k,)))
        go(c, "z1r", "z1l")

    def s4(k):
        c = copies(k)
        got(c, "z1r", "z1l")
        add((k, hi * 4 + zp, pl.ds(0, 32)), (rz1, (k, 0)))
        go(c, "z2r")
        add((k, hi * 4 + zm, pl.ds(32, 32)), (rz1, (k, 1)))
        go(c, "z2l")

    def s5(k):
        c = copies(k)
        got(c, "z2r", "z2l")
        add((k, me), (rz2, (k, 0)), (rz2, (k, 1)))
        go(c, "p1")

    def s6(k):
        c = copies(k)
        got(c, "p1")
        add((k, me, mine32), (rp1, (k,)))
        go(c, "p2r", "p2l", "p2o")

    def s7(k):
        c = copies(k)
        got(c, "p2r", "p2l", "p2o")
        total = acc[k, me, mine32, block(x)].astype(F32)
        for i in range(3):
            total = total + rp2[k, i].astype(F32)
        fin[k, fin_rows(lo), block(x)] = (total * (1.0 / 128.0)).astype(BF16)
        go(c, "p3r", "p3l", "p3o")

    def s8(k):
        c = copies(k)
        got(c, "p3r", "p3l", "p3o")
        go(c, "p4y", "p4c")

    def s9(k):
        c = copies(k)
        got(c, "p4y")
        go(c, "p5")

    def s10(k):
        got(copies(k), "p4c", "p5")

    stages = (s0, s1, s2, s3, s4, s5, s6, s7, s8, s9, s10)

    def comm(t):
        for s in range(10, -1, -1):
            k = t - RGAP * (s + 1)

            @pl.when((k >= 0) & (k < NH))
            def _():
                stages[s](k)

    def produce(k, half, a_ref, b_ref):
        slot = k % STAGED

        @pl.when(k >= STAGED)
        def _():
            copies(k - STAGED)["c"].wait_send()

        cols = pl.ds(pl.multiple_of(half * HALF, HALF), HALF)

        def body(i):
            res = tn(a_ref[:, rows_of(i, 256)], b_ref[:, cols]).astype(BF16)
            for e in range(2):
                for h in range(2):
                    first = e * 128 + h * 64
                    staged[slot, h, 2 * i + e] = res[first : first + 64]

        loop(4, body)
        copies(k)["c"].start()

    def load(m, u):
        return pltpu.make_async_copy(full.at[m], wbuf.at[u % WSLOTS], load_sem.at[u % WSLOTS])

    def bring(j):
        return (
            pltpu.make_async_copy(hid_hbm.at[j], hid_buf.at[j % 2], hid_sem.at[j % 2, 0]),
            pltpu.make_async_copy(slope_hbm.at[j], slope_buf.at[j % 2], hid_sem.at[j % 2, 1]),
        )

    def times_t(a_ref, u, write):
        def body(i):
            w = wbuf[u % WSLOTS, pl.ds(2 * i, 2)].reshape(256, D)
            write(rows_of(i, 256), nt(a_ref[...], w))

        loop(4, body)

    def bump(row, cols, rows):
        sums[row, cols] += jnp.sum(rows, axis=0, keepdims=True)

    def one(i):
        return pl.ds(i, 1)

    wide = pl.ds(0, D)
    load(WDN, 0).start()
    load(WUP, 1).start()
    load(WDN + 1, 2).start()
    for cp in bring(0):
        cp.start()
    sums[...] = jnp.zeros_like(sums)
    for s in range(8):
        vecs[:, pl.ds(s * 128, 128)] = sm_all[s].astype(F32)

    def prepare(i):
        r = rows_of(i, 32)
        rows = cot[r, :]
        cot_b[r, :] = rows.astype(BF16)
        bump(one(DB), wide, rows)

    loop(10, prepare)
    dact[...] = jnp.zeros_like(dact)
    iota_row = lax.broadcasted_iota(jnp.int32, (SEQ, SEQ), 0)
    iota_col = lax.broadcasted_iota(jnp.int32, (SEQ, SEQ), 1)
    dist[...] = (iota_row - iota_col).astype(F32)
    greet(peers, ("xr", "xl", "xo", "zr", "zl", "zo", "cross", "ylo", "yo", "core"))

    def ffn_first(j):
        for cp in bring(j):
            cp.wait()

        @pl.when(j < 3)
        def _():
            for cp in bring(j + 1):
                cp.start()

        load(WDN, 2 * j).wait()

        def write(cols, res):
            res = res * slope_buf[j % 2, :, cols]
            dub[:, cols] = res.astype(BF16)
            bump(one(UB + j), cols, res)

        times_t(cot_b, 2 * j, write)

        @pl.when(j < 3)
        def _():
            load(WUP + j + 1, 2 * j + 3).start()

        @pl.when(j == 3)
        def _():
            load(WV, 9).start()

    def ffn_second(j):
        load(WUP, 2 * j + 1).wait()

        def write(cols, res):
            dact[:, cols] += res

        times_t(dub, 2 * j + 1, write)

        @pl.when(j < 2)
        def _():
            load(WDN + j + 2, 2 * j + 4).start()

        @pl.when(j == 2)
        def _():
            load(WO, 8).start()

        @pl.when(j == 3)
        def _():
            load(WK, 10).start()

    def back(e, n):
        return e - jnp.mean(e, axis=-1, keepdims=True) - n * jnp.mean(e * n, axis=-1, keepdims=True)

    def norm_two(i):
        r = rows_of(i, 32)
        e, n, s = dact[r, :], n2[r, pl.ds(0, D)], n2[r, pl.ds(D, 128)][:, 0:1]
        bump(one(LN2G), wide, e * n)
        bump(one(LN2B), wide, e)
        m = cot[r, :] + s * back(e * vecs[LN2G : LN2G + 1, :], n)
        dmid[r, :] = m
        dmid_b[r, :] = m.astype(BF16)
        bump(one(OB), wide, m)

    def context():
        load(WO, 8).wait()

        def write(cols, res):
            dctx[:, cols] = res.astype(BF16)

        times_t(dmid_b, 8, write)
        load(WQ, 11).start()

    scale = HEAD_DIM**-0.5

    def attend_back(p, factor):
        lane = lax.broadcasted_iota(jnp.int32, (SEQ, 128), 1)
        lane_row = lax.broadcasted_iota(jnp.int32, (SEQ, 128), 1)
        cols = pl.ds(pl.multiple_of(p * 128, 128), 128)
        q_pair, k_pair, v_pair = qkv[0, :, cols], qkv[1, :, cols], qkv[2, :, cols]
        c_pair = dctx[:, cols]
        out = []
        for e in range(2):
            mine = (lane < 64) if e == 0 else (lane >= 64)
            zero = jnp.zeros_like(q_pair)
            s = nt(jnp.where(mine, q_pair, zero), k_pair)
            d = dist[...]
            s = jnp.where(d >= 0.0, s * scale - (factor * slope_of(e)) * d, -jnp.inf)
            total = jnp.sum(
                jnp.where(lane_row == 2 * p + e, lse[...], 0.0), axis=-1, keepdims=True
            )
            prob = jnp.exp(s - total)
            d_prob = nt(jnp.where(mine, c_pair, zero), v_pair)
            d_score = prob * (d_prob - jnp.sum(prob * d_prob, axis=-1, keepdims=True))
            d_score = d_score.astype(BF16)
            out.append((nn(d_score, k_pair), tn(d_score, q_pair), tn(prob.astype(BF16), c_pair)))
        low = lane < 64
        g_q = jnp.where(low, out[0][0], out[1][0]) * scale
        g_k = jnp.where(low, out[0][1], out[1][1]) * scale
        g_v = jnp.where(low, out[0][2], out[1][2])
        dqkv[2, :, cols], dqkv[1, :, cols], dqkv[0, :, cols] = (
            g_q.astype(BF16),
            g_k.astype(BF16),
            g_v.astype(BF16),
        )
        bump(one(QB), cols, g_q)
        bump(one(VB), cols, g_v)
        return factor * 0.5

    def first_grad(i):
        load(WV, 9 + i).wait()

        def write(cols, res):
            @pl.when(i == 0)
            def _():
                dact[:, cols] = res

            @pl.when(i > 0)
            def _():
                dact[:, cols] += res

        times_t(dqkv.at[i], 9 + i, write)

    def norm_one(i):
        r = rows_of(i, 32)
        n, s = center_scale(x_in[r, :].astype(F32))
        e = dact[r, :]
        bump(one(LN1G), wide, e * n)
        bump(one(LN1B), wide, e)
        input_grad[r, :] = dmid[r, :] + s * back(e * vecs[LN1G : LN1G + 1, :], n)

    rounds = (
        (core, 2, ("core",)),
        (x, 4, ("xr", "xl", "xo")),
        (hi * 2 + lo, 4, ("ylo", "cross", "yo")),
        (z, 4, ("zr", "zl", "zo")),
    )

    def small_copies(i):
        mine, n, to = rounds[i]
        view = small_in.at[i, mine]
        return [
            remote(view, view, sm_send.at[i, m], sm_recv.at[i, m], name)
            for m, name in enumerate(to)
        ]

    def small_round(i):
        if i == 0:
            small_in[0, core] = sums[...].astype(BF16)
        else:
            for cp in small_copies(i - 1):
                cp.wait_recv()
            total = small_in[i - 1, 0].astype(F32)
            for m in range(1, rounds[i - 1][1]):
                total = total + small_in[i - 1, m].astype(F32)
            if i < 4:
                small_in[i, rounds[i][0]] = total.astype(BF16)
            else:
                sums[...] = total * (1.0 / 128.0)
        if i < 4:
            for cp in small_copies(i):
                cp.start()

    def slot(t):
        comm(t)
        j, w, half = t // 4, (t // 2) % 2, t % 2

        @pl.when((t < 16) & (t % 4 == 0))
        def _():
            ffn_first(j)

        @pl.when((t < 16) & (w == 0))
        def _():
            produce(t, half, hid_buf.at[j % 2], cot_b)

        @pl.when((t < 16) & (w == 1))
        def _():
            produce(t, half, act2, dub)

        @pl.when((t < 16) & (t % 4 == 3))
        def _():
            ffn_second(j)

        @pl.when(t == 16)
        def _():
            loop(10, norm_two)

        @pl.when((t >= 16) & (t < 18))
        def _():
            produce(t, half, ctx, dmid_b)

        @pl.when(t == 17)
        def _():
            context()

        @pl.when((t >= 18) & (t < 20))
        def _():
            first = jnp.where(t == 18, 1.0, 0.0625).astype(F32)
            lax.fori_loop(0, 4, lambda p, f: attend_back((t - 18) * 4 + p, f), first)

        @pl.when((t >= 18) & (t < 24))
        def _():
            produce(t, (t - 18) // 3, act1, dqkv.at[(t - 18) % 3])

        @pl.when((t >= 24) & (t < 27))
        def _():
            first_grad(t - 24)

        @pl.when(t == 27)
        def _():
            loop(10, norm_one)

        for i in range(5):

            @pl.when(t == 28 + RGAP * i)
            def _():
                small_round(i)

    loop(NH + RGAP * 11, slot)
    fin_small[...] = sums[:, pl.ds(pl.multiple_of(me * 128, 128), 128)]
    for k in range(NH):
        m, half = MADE[k]
        cols = pl.ds(half * HALF, HALF)
        if m < WO:
            out_qkv[:, pl.ds(m * D + half * HALF, HALF)] = fin[k]
        elif m == WO:
            out_o[:, cols] = fin[k]
        elif m < WDN:
            for s in range(4):
                first = (half * 4 + s) * 512 + (m - WUP) * 128
                out_up[:, pl.ds(first, 128)] = fin[k, :, pl.ds(s * 128, 128)]
        else:
            out_down[pl.ds((m - WDN) * 128, 128), cols] = fin[k]

    def sent(k):
        c = copies(k)
        for name in c:
            if name != "c":
                c[name].wait_send()

        @pl.when(k >= NH - STAGED)
        def _():
            c["c"].wait_send()

    loop(NH, sent)
    for i in range(4):
        for cp in small_copies(i):
            cp.wait_send()


def backward_reduce(full, hid, slope, sm, x_in, cot, act1, qkv, lse, ctx, act2, n2):
    vm = pl.BlockSpec(memory_space=pltpu.VMEM)
    hbm = pl.BlockSpec(memory_space=pl.ANY)
    S = jax.ShapeDtypeStruct
    V = pltpu.VMEM
    dma = pltpu.SemaphoreType.DMA
    return pl.pallas_call(
        backward_kernel,
        out_shape=[
            S((SEQ, D), F32),
            S((128, 3 * D), BF16),
            S((128, D), BF16),
            S((128, 4 * D), BF16),
            S((512, D), BF16),
            S((16, 128), F32),
        ],
        in_specs=[hbm] * 3 + [vm] * 9,
        out_specs=[vm] * 6,
        scratch_shapes=[
            V((NH, 8, 64, HALF), BF16),
            V((STAGED, 2, 8, 64, HALF), BF16),
            V((NH, 2, 2, 16, HALF), BF16),
            V((NH, 2, 4, 16, HALF), BF16),
            V((NH, 4, 16, HALF), BF16),
            V((NH, 2, 32, HALF), BF16),
            V((NH, 2, 64, HALF), BF16),
            V((NH, 32, HALF), BF16),
            V((NH, 3, 32, 128), BF16),
            V((NH, 128, HALF), BF16),
            V((WSLOTS, 8, 128, D), BF16),
            V((2, SEQ, D), BF16),
            V((2, SEQ, D), F32),
            V((SEQ, D), BF16),
            V((SEQ, D), BF16),
            V((SEQ, D), F32),
            V((SEQ, D), F32),
            V((SEQ, D), BF16),
            V((SEQ, D), BF16),
            V((3, SEQ, D), BF16),
            V((SEQ, SEQ), F32),
            V((16, D), F32),
            V((16, D), F32),
            V((4, 4, 16, D), BF16),
            dma((NH, RCOPIES)),
            dma((NH, RCOPIES)),
            dma((WSLOTS,)),
            dma((2, 2)),
            dma((4, 3)),
            dma((4, 3)),
        ],
        compiler_params=pltpu.CompilerParams(
            collective_id=1, has_side_effects=True, vmem_limit_bytes=63 * MIB
        ),
        name="backward_reduce",
    )(full, hid, slope, sm, x_in, cot, act1, qkv, lse, ctx, act2, n2)


def on_device(
    x_in,
    cotangent,
    ln1_gain,
    ln1_bias,
    w_qkv,
    q_bias,
    v_bias,
    w_attn_out,
    out_bias,
    ln2_gain,
    ln2_bias,
    w_up,
    up_bias,
    w_down,
    down_bias,
):
    rows = (ln1_gain, ln1_bias, q_bias, v_bias, out_bias, ln2_gain, ln2_bias, down_bias)
    small = jnp.pad(up_bias.reshape(4, 128), ((UB, 4), (0, 0)))
    for i, row in enumerate(rows):
        small = small + jnp.pad(row.reshape(1, 128), ((i, 15 - i), (0, 0)))
    full, sm, block_out, act1, qkv, lse, ctx, act2, n2, hid, slope = gather_forward(
        w_qkv, w_attn_out, w_up, w_down, small, x_in
    )
    input_grad, g_qkv, g_o, g_up, g_down, vals = backward_reduce(
        full, hid, slope, sm, x_in, cotangent, act1, qkv, lse, ctx, act2, n2
    )
    return (
        block_out,
        input_grad,
        vals[LN1G],
        vals[LN1B],
        g_qkv.astype(F32),
        vals[QB],
        vals[VB],
        g_o.astype(F32),
        vals[OB],
        vals[LN2G],
        vals[LN2B],
        g_up.astype(F32),
        vals[UB : UB + 4].reshape(-1),
        g_down.astype(F32),
        vals[DB],
    )


def solution(mesh):
    placed = (
        P(("rep", "shard"), None),
        P(("rep", "shard"), None),
        P("shard"),
        P("shard"),
        P("shard", None),
        P("shard"),
        P("shard"),
        P("shard", None),
        P("shard"),
        P("shard"),
        P("shard"),
        P("shard", None),
        P("shard"),
        P("shard", None),
        P("shard"),
    )
    return jax.shard_map(
        on_device,
        mesh=mesh,
        in_specs=placed,
        out_specs=(
            P(("rep", "shard"), None),
            P(("rep", "shard"), None),
            P("shard"),
            P("shard"),
            P("shard", None),
            P("shard"),
            P("shard"),
            P("shard", None),
            P("shard"),
            P("shard"),
            P("shard"),
            P("shard", None),
            P("shard"),
            P("shard", None),
            P("shard"),
        ),
        check_vma=False,
    )
```

profile of v0, /device:TPU:1, one launch (start us, length us, event | category | flops | bytes accessed | tf_op | source)
XLA Modules:
  0.0 254.2 jit_solution(2898580312946732079)
XLA Ops:
  0.6 1.4 pad_add_fusion.refs_4_
  2.1 100.5 %gather_forward.1 = (bf16[12,8,128,1024]{3,2,1,0:T(8,128)(2,1)}, bf16[8,16,128]{2,1,0:T(8,128)(2,1)}, bf16[320,1024]{1,0:T(8,128)(2,1)}, bf16[320,1024]{1,0:T(8,...) custom-call(bf16[128,3072]{1,0:T(8,128)(2,1)} %refs_0_.1, ...), custom_call_target="tpu_custom_call" | custom-call | tf_op jit(solution)/shard_map/gather_forward/pallas_call | solution.py:442
  102.6 139.5 %backward_reduce.1 = (f32[320,1024]{1,0:T(8,128)}, bf16[128,3072]{1,0:T(8,128)(2,1)}, bf16[128,1024]{1,0:T(8,128)(2,1)}, bf16[128,4096]{1,0:T(8,128)(2,1)}, bf16...) custom-call(bf16[12,8,128,1024]{3,2,1,0:T(8,128)(2,1)} %get-tuple-element.33.refs_0_, ...), custom_call_target="tpu_custom_call" | custom-call | tf_op jit(solution)/shard_map/backward_reduce/pallas_call | solution.py:977
  242.1 0.0 copy-start.2
  242.1 1.3 slice_bitcast_fusion
  243.4 1.5 slice_bitcast_fusion.1
  244.9 1.8 convert_element_type.31
  246.7 2.4 convert_element_type.30
  249.2 0.0 copy-done.2
  249.2 0.0 copy-start.1
  249.2 1.5 convert_element_type.32
  250.7 0.0 copy-done.1
  250.7 0.0 copy-start.3
  250.7 0.0 copy-start
  250.7 1.6 convert_element_type.33
  252.3 0.0 copy-done.3
  252.3 0.8 copy.32
  253.1 0.0 copy-done
  253.1 1.1 copy.33
Async XLA Ops:
  242.1 7.1 %copy-start.2 = (bf16[128,4096]{1,0:T(8,128)(2,1)S(1)}, bf16[128,4096]{1,0:T(8,128)(2,1)}, u32[]{:S(2)}) copy-start(bf16[128,4096]{1,0:T(8,128)(2,1)} %get-tuple-element.47) | copy-start | bytes 3145732
  249.2 1.5 copy-start.1
  250.7 1.6 copy-start.3
  250.7 2.4 copy-start
where the time goes:
time: 254 us
  Pallas kernels  240 us (94%)
  other arithmetic  8.73 us (3%)
  local copies, waits for them, and re-layouts  4.77 us (2%)
    pallas_call x1, Pallas kernels, backward_reduce(): pl.pallas_call(backward_kernel, out_shape=[S((SEQ, D), F32), S((128, 3 *...  139 us
    pallas_call x1, Pallas kernels, gather_forward(): pl.pallas_call(forward_kernel, out_shape=[S((NCH, 8, 128, D), BF16), S((8...  101 us

commit v1 on v0

--- a/solution.py
+++ b/solution.py
@@ -109,7 +109,8 @@
     w_qkv, w_o, w_up, w_down, small, x_in = refs[:6]
     full_out, sm_all, block_out, act1_o, qkv_o, lse, ctx_o, act2_o, n2_o, hid_o, slope_o = refs[6:17]
     full, act1, qkv, ctx, act2, n2, hid, slope, mid, dist, vecs, qkv_bias = refs[17:29]
-    send_sem, recv_sem, own_sem, out_sem, sm_send, sm_recv, save_sem = refs[29:]
+    act1_t, ctx_t, act2_t, hid_t = refs[29:33]
+    send_sem, recv_sem, own_sem, out_sem, sm_send, sm_recv, save_sem = refs[33:]
     x, core, hi, z, peers = place()
     other = 1 - hi
     me = hi * 4 + z
@@ -144,37 +145,43 @@
     others = pl.ds(other * 4, 4)
     sx = lambda i: base + ((x + i) % 4) * 16
 
+    def table(m, cols):
+        def view(which, first, count):
+            return full.at[m, which, pl.ds(pl.multiple_of(first, 16), count), cols]
+
+        return (
+            ("z1r", view(me, base, 64), "zr", 0),
+            ("z1l", view(me, base, 64), "zl", 1),
+            ("y0", view(me, quarter, 16), "cross", 2),
+            ("z2r", view(left, base, 32), "zr", 3),
+            ("y1", view(left, quarter, 16), "cross", 2),
+            ("c1", view(left, base, 64), "core", 8),
+            ("z2l", view(right, base + 32, 32), "zl", 4),
+            ("y2", view(right, quarter, 16), "cross", 2),
+            ("c2", view(right, base, 64), "core", 8),
+            ("y3", view(far, quarter, 16), "cross", 2),
+            ("c3", view(far, base, 64), "core", 8),
+            ("x1r", view(others, quarter, 16), "xr", 5),
+            ("x1l", view(others, quarter, 16), "xl", 6),
+            ("c4", view(others, quarter, 16), "core", 8),
+            ("x2r", view(pl.ds(other * 4, 2), sx(3), 16), "xr", 7),
+            ("c5", view(others, sx(3), 16), "core", 8),
+            ("x2l", view(pl.ds(other * 4 + 2, 2), sx(1), 16), "xl", 9),
+            ("c6", view(others, sx(1), 16), "core", 8),
+            ("c7", view(others, sx(2), 16), "core", 8),
+        )
+
     def copies(k):
         cols = pl.ds(pl.multiple_of((k % 2) * HALF, HALF), HALF)
-
-        def view(which, first, count):
-            return full.at[k // 2, which, pl.ds(pl.multiple_of(first, 16), count), cols]
-
-        table = (
-            ("z1r", view(me, base, 64), "zr"),
-            ("z1l", view(me, base, 64), "zl"),
-            ("y0", view(me, quarter, 16), "cross"),
-            ("z2r", view(left, base, 32), "zr"),
-            ("y1", view(left, quarter, 16), "cross"),
-            ("c1", view(left, base, 64), "core"),
-            ("z2l", view(right, base + 32, 32), "zl"),
-            ("y2", view(right, quarter, 16), "cross"),
-            ("c2", view(right, base, 64), "core"),
-            ("y3", view(far, quarter, 16), "cross"),
-            ("c3", view(far, base, 64), "core"),
-            ("x1r", view(others, quarter, 16), "xr"),
-            ("x1l", view(others, quarter, 16), "xl"),
-            ("c4", view(others, quarter, 16), "core"),
-            ("x2r", view(pl.ds(other * 4, 2), sx(3), 16), "xr"),
-            ("c5", view(others, sx(3), 16), "core"),
-            ("x2l", view(pl.ds(other * 4 + 2, 2), sx(1), 16), "xl"),
-            ("c6", view(others, sx(1), 16), "core"),
-            ("c7", view(others, sx(2), 16), "core"),
-        )
-        return {
-            name: remote(v, v, send_sem.at[k, i], recv_sem.at[k, i], to)
-            for i, (name, v, to) in enumerate(table)
+        made = {
+            name: remote(v, v, send_sem.at[i], recv_sem.at[k, r], to)
+            for i, (name, v, to, r) in enumerate(table(k // 2, cols))
         }
+        quarters = full.at[k // 2, others, pl.ds(pl.multiple_of(quarter, 16), 16), cols]
+        made["y"] = remote(quarters, quarters, send_sem.at[2], recv_sem.at[k, 2], "cross")
+        seven = full.at[k // 2, pl.ds(0, 7), pl.ds(pl.multiple_of(base, 64), 64), cols]
+        made["c"] = remote(seven, seven, send_sem.at[5], recv_sem.at[k, 8], "core")
+        return made
 
     def stage(waits, sends):
         def run(k):
@@ -206,7 +213,7 @@
         return pltpu.make_async_copy(full.at[m], full_out.at[m], out_sem.at[m])
 
     def stage6(k):
-        stage(("c1", "c2", "c3", "c4", "c5", "c6", "c7"), ())(k)
+        stage(("c",), ())(k)
 
         @pl.when(k % 2 == 1)
         def _():
@@ -216,7 +223,7 @@
         stage0,
         stage1,
         stage(("z2r", "z2l"), ("y3", "c3")),
-        stage(("y0", "y1", "y2", "y3"), ("x1r", "x1l", "c4")),
+        stage(("y",), ("x1r", "x1l", "c4")),
         stage4,
         stage(("x2r", "x2l"), ("c7",)),
         stage6,
@@ -244,12 +251,18 @@
         return pltpu.make_async_copy(src, dst, save_sem.at[i])
 
     saves = [
-        save(0, act1, act1_o),
+        save(0, act1_t, act1_o),
         save(1, qkv, qkv_o),
-        save(2, ctx, ctx_o),
-        save(3, act2, act2_o),
+        save(2, ctx_t, ctx_o),
+        save(3, act2_t, act2_o),
         save(4, n2, n2_o),
     ]
+
+    def turn(src, dst):
+        def body(i):
+            dst[rows_of(i, 256), :] = src[:, rows_of(i, 256)].T
+
+        loop(4, body)
 
     def norm_one():
         for s in range(8):
@@ -267,6 +280,7 @@
         row = lax.broadcasted_iota(jnp.int32, (SEQ, SEQ), 0)
         col = lax.broadcasted_iota(jnp.int32, (SEQ, SEQ), 1)
         dist[...] = (row - col).astype(F32)
+        turn(act1, act1_t)
         saves[0].start()
 
     def matmul(a_ref, k, write):
@@ -312,6 +326,7 @@
         lax.fori_loop(0, 4, lambda p, f: attend(i * 4 + p, f), first)
 
     def out_proj():
+        turn(ctx, ctx_t)
         saves[2].start()
 
         def body(k):
@@ -330,12 +345,13 @@
             act2[r, :] = (n * vec(LN2G) + vec(LN2B)).astype(BF16)
 
         loop(10, norm)
+        turn(act2, act2_t)
         saves[3].start()
         saves[4].start()
 
     def save_up(j):
         return (
-            pltpu.make_async_copy(hid.at[j], hid_o.at[j], save_sem.at[5 + j]),
+            pltpu.make_async_copy(hid_t.at[j], hid_o.at[j], save_sem.at[5 + j]),
             pltpu.make_async_copy(slope.at[j], slope_o.at[j], save_sem.at[9 + j]),
         )
 
@@ -344,7 +360,9 @@
 
         def write(cols, res):
             value, grad = gelu_both(res + vecs[pl.ds(UB + j, 1), cols])
-            hid[j, :, cols] = value.astype(BF16)
+            value = value.astype(BF16)
+            hid[j, :, cols] = value
+            hid_t[j, cols, :] = value.T
             slope[j, :, cols] = grad
 
         matmul(act2, k, write)
@@ -416,11 +434,8 @@
 
     loop(NH + 6 * GAP, slot)
 
-    def sent(k):
-        for cp in copies(k).values():
-            cp.wait_send()
-
-    loop(NH, sent)
+    for i, (name, v, to, r) in enumerate(table(pl.ds(0, NCH), wide)):
+        remote(v, v, send_sem.at[i], recv_sem.at[0, r], to).wait_send()
     for cp in sm_copy:
         cp.wait_send()
     for m in range(NCH):
@@ -438,20 +453,20 @@
     S = jax.ShapeDtypeStruct
     V = pltpu.VMEM
     dma = pltpu.SemaphoreType.DMA
-    act = S((SEQ, D), BF16)
+    act, turned = S((SEQ, D), BF16), S((D, SEQ), BF16)
     return pl.pallas_call(
         forward_kernel,
         out_shape=[
             S((NCH, 8, 128, D), BF16),
             S((8, 16, 128), BF16),
             act,
-            act,
+            turned,
             S((3, SEQ, D), BF16),
             S((SEQ, 128), F32),
-            act,
-            act,
+            turned,
+            turned,
             S((SEQ, D + 128), F32),
-            S((4, SEQ, D), BF16),
+            S((4, D, SEQ), BF16),
             S((4, SEQ, D), F32),
         ],
         in_specs=[hbm] * 4 + [vm] * 2,
@@ -469,8 +484,12 @@
             V((SEQ, SEQ), F32),
             V((16, D), F32),
             V((8, D), F32),
-            dma((NH, GCOPIES)),
-            dma((NH, GCOPIES)),
+            V((D, SEQ), BF16),
+            V((D, SEQ), BF16),
+            V((D, SEQ), BF16),
+            V((4, D, SEQ), BF16),
+            dma((GCOPIES,)),
+            dma((NH, 10)),
             dma((NCH,)),
             dma((NCH,)),
             dma((4,)),
@@ -501,7 +520,7 @@
     acc, staged, rx1, rx2, ry, rz1, rz2, rp1, rp2, fin = refs[18:28]
     wbuf, hid_buf, slope_buf, cot_b, dub, dact, dmid, dmid_b, dctx, dqkv, dist, vecs = refs[28:40]
     sums, small_in = refs[40:42]
-    send_sem, recv_sem, load_sem, hid_sem, sm_send, sm_recv = refs[42:]
+    send_sem, send_c, recv_sem, load_sem, hid_sem, sm_send, sm_recv = refs[42:]
     x, core, hi, z, peers = place()
     lo = (lax.axis_index("rep") // 2) % 2
     other = 1 - hi
@@ -532,12 +551,13 @@
     mine32 = pl.ds(pl.multiple_of(lo * 32, 32), 32)
     theirs32 = pl.ds(pl.multiple_of((1 - lo) * 32, 32), 32)
 
-    def copies(k):
+    def table(k):
         piece = fin.at[k, fin_rows(lo), block(x)]
         whole = fin.at[k, fin_rows(lo)]
         theirs = fin.at[k, fin_rows(1 - lo)]
-        table = (
-            ("c", staged.at[k % STAGED, 1 - core], acc.at[k], "core"),
+        slot = k % STAGED if not isinstance(k, pl.Slice) else 0
+        return (
+            ("c", staged.at[slot, 1 - core], acc.at[k], "core"),
             ("x1r", acc.at[k, pl.ds(other * 4, 2), sub(xo)], rx1.at[k, 0], "xr"),
             ("x1l", acc.at[k, pl.ds(other * 4 + 2, 2), sub(xo)], rx1.at[k, 1], "xl"),
             ("x2r", acc.at[k, others, sub(xp)], rx2.at[k, 0], "xr"),
@@ -558,9 +578,13 @@
             ("p4c", whole, whole, "core"),
             ("p5", theirs, theirs, "core"),
         )
+
+    def copies(k):
         return {
-            name: remote(src, dst, send_sem.at[k, i], recv_sem.at[k, i], to)
-            for i, (name, src, dst, to) in enumerate(table)
+            name: remote(
+                src, dst, send_c.at[k % STAGED] if name == "c" else send_sem.at[i], recv_sem.at[k, i], to
+            )
+            for i, (name, src, dst, to) in enumerate(table(k))
         }
 
     def got(c, *names):
@@ -669,7 +693,7 @@
         cols = pl.ds(pl.multiple_of(half * HALF, HALF), HALF)
 
         def body(i):
-            res = tn(a_ref[:, rows_of(i, 256)], b_ref[:, cols]).astype(BF16)
+            res = nn(a_ref[rows_of(i, 256), :], b_ref[:, cols]).astype(BF16)
             for e in range(2):
                 for h in range(2):
                     first = e * 128 + h * 64
@@ -952,17 +976,11 @@
         else:
             out_down[pl.ds((m - WDN) * 128, 128), cols] = fin[k]
 
-    def sent(k):
-        c = copies(k)
-        for name in c:
-            if name != "c":
-                c[name].wait_send()
-
-        @pl.when(k >= NH - STAGED)
-        def _():
-            c["c"].wait_send()
-
-    loop(NH, sent)
+    for i, (name, src, dst, to) in enumerate(table(pl.ds(0, NH))):
+        if name != "c":
+            remote(src, dst, send_sem.at[i], recv_sem.at[0, i], to).wait_send()
+    for k in range(NH - STAGED, NH):
+        copies(k)["c"].wait_send()
     for i in range(4):
         for cp in small_copies(i):
             cp.wait_send()
@@ -998,7 +1016,7 @@
             V((NH, 3, 32, 128), BF16),
             V((NH, 128, HALF), BF16),
             V((WSLOTS, 8, 128, D), BF16),
-            V((2, SEQ, D), BF16),
+            V((2, D, SEQ), BF16),
             V((2, SEQ, D), F32),
             V((SEQ, D), BF16),
             V((SEQ, D), BF16),
@@ -1011,7 +1029,8 @@
             V((16, D), F32),
             V((16, D), F32),
             V((4, 4, 16, D), BF16),
-            dma((NH, RCOPIES)),
+            dma((RCOPIES,)),
+            dma((STAGED,)),
             dma((NH, RCOPIES)),
             dma((WSLOTS,)),
             dma((2, 2)),

time: 254 us -> 242 us (0.953)
  Pallas kernels: 240 us -> 228 us
    pallas_call x1, Pallas kernels: 139 us -> 133 us  [backward_reduce(): pl.pallas_call(backward_kernel, out_shape=[S((SEQ, D), F32), S((128, 3 *...]
    pallas_call x1, Pallas kernels: 101 us -> 95.2 us  [gather_forward(): pl.pallas_call(forward_kernel, out_shape=[S((NCH, 8, 128, D), BF16), S((8...]
where the time goes in v1:
time: 242 us
  Pallas kernels  228 us (94%)
  other arithmetic  8.73 us (4%)
  local copies, waits for them, and re-layouts  4.76 us (2%)
    pallas_call x1, Pallas kernels, backward_reduce(): pl.pallas_call(backward_kernel, out_shape=[S((SEQ, D), F32), S((128, 3 *...  133 us
    pallas_call x1, Pallas kernels, gather_forward(): pl.pallas_call(forward_kernel, out_shape=[S((NCH, 8, 128, D), BF16), S((8...  95.2 us

profile of v1, /device:TPU:1, one launch (start us, length us, event | category | flops | bytes accessed | tf_op | source)
XLA Modules:
  0.0 242.0 jit_solution(1605821681256097975)
XLA Ops:
  0.6 1.4 pad_add_fusion.refs_4_
  2.1 95.2 %gather_forward.1 = (bf16[12,8,128,1024]{3,2,1,0:T(8,128)(2,1)}, bf16[8,16,128]{2,1,0:T(8,128)(2,1)}, bf16[320,1024]{1,0:T(8,128)(2,1)}, bf16[1024,320]{1,0:T(8,...) custom-call(bf16[128,3072]{1,0:T(8,128)(2,1)} %refs_0_.1, ...), custom_call_target="tpu_custom_call" | custom-call | tf_op jit(solution)/shard_map/gather_forward/pallas_call | solution.py:457
  97.3 132.7 %backward_reduce.1 = (f32[320,1024]{1,0:T(8,128)}, bf16[128,3072]{1,0:T(8,128)(2,1)}, bf16[128,1024]{1,0:T(8,128)(2,1)}, bf16[128,4096]{1,0:T(8,128)(2,1)}, bf16...) custom-call(bf16[12,8,128,1024]{3,2,1,0:T(8,128)(2,1)} %get-tuple-element.33.refs_0_, ...), custom_call_target="tpu_custom_call" | custom-call | tf_op jit(solution)/shard_map/backward_reduce/pallas_call | solution.py:995
  230.0 0.0 copy-start.2
  230.0 1.3 slice_bitcast_fusion
  231.3 1.5 slice_bitcast_fusion.1
  232.8 1.8 convert_element_type.31
  234.6 2.4 %convert_element_type.30 = f32[128,3072]{1,0:T(8,128)} convert(bf16[128,3072]{1,0:T(8,128)(2,1)} %get-tuple-element.45) | non-fusion elementwise | flops 393216 | bytes 2359296 | tf_op jit(solution)/shard_map/convert_element_type | solution.py:1079
  237.0 0.0 copy-done.2
  237.0 0.0 copy-start.1
  237.1 1.5 convert_element_type.32
  238.6 0.0 copy-done.1
  238.6 0.0 copy-start.3
  238.6 0.0 copy-start
  238.6 1.6 convert_element_type.33
  240.2 0.0 copy-done.3
  240.2 0.8 copy.32
  241.0 0.0 copy-done
  241.0 1.1 copy.33
Async XLA Ops:
  230.0 7.1 %copy-start.2 = (bf16[128,4096]{1,0:T(8,128)(2,1)S(1)}, bf16[128,4096]{1,0:T(8,128)(2,1)}, u32[]{:S(2)}) copy-start(bf16[128,4096]{1,0:T(8,128)(2,1)} %get-tuple-element.47) | copy-start | bytes 3145732
  237.0 1.5 copy-start.1
  238.6 1.6 copy-start.3
  238.6 2.4 copy-start

commit v2 on v1

--- a/solution.py
+++ b/solution.py
@@ -102,7 +102,7 @@
 HALF = 512
 NH = 24
 GCOPIES = 20
-GAP = 3
+GAP = 2
 
 
 def forward_kernel(*refs):
@@ -230,7 +230,7 @@
     )
 
     def comm(t):
-        for s in range(6, -1, -1):
+        for s in range(7):
             k = t - GAP * s
 
             @pl.when((k >= 0) & (k < NH))
@@ -676,7 +676,7 @@
     stages = (s0, s1, s2, s3, s4, s5, s6, s7, s8, s9, s10)
 
     def comm(t):
-        for s in range(10, -1, -1):
+        for s in range(11):
             k = t - RGAP * (s + 1)
 
             @pl.when((k >= 0) & (k < NH))

time: 242 us -> 238 us (0.983)
  Pallas kernels: 228 us -> 224 us
    pallas_call x1, Pallas kernels: 133 us -> 130 us  [backward_reduce(): pl.pallas_call(backward_kernel, out_shape=[S((SEQ, D), F32), S((128, 3 *...]
where the time goes in v2:
time: 238 us
  Pallas kernels  224 us (94%)
  other arithmetic  8.73 us (4%)
  local copies, waits for them, and re-layouts  4.76 us (2%)
    pallas_call x1, Pallas kernels, backward_reduce(): pl.pallas_call(backward_kernel, out_shape=[S((SEQ, D), F32), S((128, 3 *...  130 us
    pallas_call x1, Pallas kernels, gather_forward(): pl.pallas_call(forward_kernel, out_shape=[S((NCH, 8, 128, D), BF16), S((8...  93.9 us

profile of v2, /device:TPU:1, one launch (start us, length us, event | category | flops | bytes accessed | tf_op | source)
XLA Modules:
  0.0 238.1 jit_solution(12074962801879593314)
XLA Ops:
  0.6 1.4 pad_add_fusion.refs_4_
  2.1 93.9 %gather_forward.1 = (bf16[12,8,128,1024]{3,2,1,0:T(8,128)(2,1)}, bf16[8,16,128]{2,1,0:T(8,128)(2,1)}, bf16[320,1024]{1,0:T(8,128)(2,1)}, bf16[1024,320]{1,0:T(8,...) custom-call(bf16[128,3072]{1,0:T(8,128)(2,1)} %refs_0_.1, ...), custom_call_target="tpu_custom_call" | custom-call | tf_op jit(solution)/shard_map/gather_forward/pallas_call | solution.py:457
  95.9 130.1 %backward_reduce.1 = (f32[320,1024]{1,0:T(8,128)}, bf16[128,3072]{1,0:T(8,128)(2,1)}, bf16[128,1024]{1,0:T(8,128)(2,1)}, bf16[128,4096]{1,0:T(8,128)(2,1)}, bf16...) custom-call(bf16[12,8,128,1024]{3,2,1,0:T(8,128)(2,1)} %get-tuple-element.33.refs_0_, ...), custom_call_target="tpu_custom_call" | custom-call | tf_op jit(solution)/shard_map/backward_reduce/pallas_call | solution.py:995
  226.1 0.0 copy-start.2
  226.1 1.3 slice_bitcast_fusion
  227.4 1.5 slice_bitcast_fusion.1
  228.9 1.8 convert_element_type.31
  230.7 2.4 %convert_element_type.30 = f32[128,3072]{1,0:T(8,128)} convert(bf16[128,3072]{1,0:T(8,128)(2,1)} %get-tuple-element.45) | non-fusion elementwise | flops 393216 | bytes 2359296 | tf_op jit(solution)/shard_map/convert_element_type | solution.py:1079
  233.1 0.0 copy-done.2
  233.1 0.0 copy-start.1
  233.1 1.5 convert_element_type.32
  234.7 0.0 copy-done.1
  234.7 0.0 copy-start.3
  234.7 0.0 copy-start
  234.7 1.6 convert_element_type.33
  236.2 0.0 copy-done.3
  236.2 0.8 copy.32
  237.1 0.0 copy-done
  237.1 1.1 copy.33
Async XLA Ops:
  226.1 7.1 %copy-start.2 = (bf16[128,4096]{1,0:T(8,128)(2,1)S(1)}, bf16[128,4096]{1,0:T(8,128)(2,1)}, u32[]{:S(2)}) copy-start(bf16[128,4096]{1,0:T(8,128)(2,1)} %get-tuple-element.47) | copy-start | bytes 3145732
  233.1 1.5 copy-start.1
  234.7 1.6 copy-start.3
  234.7 2.4 %copy-start = (f32[320,1024]{1,0:T(8,128)S(1)}, f32[320,1024]{1,0:T(8,128)}, u32[]{:S(2)}) copy-start(f32[320,1024]{1,0:T(8,128)} %get-tuple-element.73) | copy-start | bytes 3932164
